TPU v7x, 256 devices: a whole 4x4x8 slice. The times are simulated.
256 devices in a mesh: pipe: 16 (over z, core), dp: 4 (over x), tensor: 4 (over y).
Axes of the slice: x: 4, y: 4, z: 8, core: 2. Of those that a mesh axis runs over, the one named last changes fastest.
Arguments:
- acts: bfloat16 [16, 2048, 8192], P('pipe', 'dp', 'tensor'), may hold values from -6 to 6
- grads: bfloat16 [16, 2048, 8192], P('pipe', 'dp', 'tensor'), may hold values from -6 to 6
- sketch_index: int32 [16, 2, 16], P('pipe'), may hold values from 0 to 63, as said below
- sketch_values: bfloat16 [16, 2, 16, 128, 32], P('pipe'), may hold values from -0.125 to 0.125
Outputs:
- basis: float32 [16384, 256], P(('pipe', 'tensor'), 'dp')
Inputs may be any that keep to these rules, and one draw needn't show every extreme that they name: `sketch_index`: the 16 blocks of each sketch are distinct.
All inputs are finite; a program needn't handle non-finite values.
Results may differ from a plain program's by a relative error of at most 0.0003.
Values sent between devices are 32-bit elements; how exact they have to be, the bound alone decides.
A program may use at most 64 MiB of HBM per device.

v0:
```python
import jax
import jax.numpy as jnp
from jax import lax
from jax.sharding import PartitionSpec as P

RANK = 256
ITERS = 2
TOK_EX = 4


def from_partner(block, axis, apart):
    count = lax.axis_size(axis)
    route = []
    for low in range(count):
        high = low | 1 << apart
        if high != low and high < count:
            route += [(low, high), (high, low)]
    return lax.ppermute(block, axis, route)


def mm(a, b):
    return jnp.matmul(a, b, precision=lax.Precision.HIGHEST)


def layer_total(value):
    return lax.psum(value, "pipe")


def orthonormal(block, total):
    lower = jnp.linalg.cholesky(total(mm(block.T, block)))
    return lax.linalg.triangular_solve(lower, block, left_side=False, lower=True, transpose_a=True)


def reduce_plain(joined, total):
    q_basis = orthonormal(joined[:, :RANK] + joined[:, RANK:], total)
    for turn in range(ITERS):
        q_basis = orthonormal(mm(joined, total(mm(joined.T, q_basis))), total)
    weights = total(mm(joined.T, q_basis))
    lower = jnp.linalg.cholesky(mm(weights.T, weights))
    return mm(q_basis, lower)


def shards(acts, grads, sketch_index, sketch_values):
    local_width = acts.shape[2]
    blocks = local_width // 128
    width = sketch_values.shape[4]
    tensor_pos = lax.axis_index("tensor")
    tensor_count = lax.axis_size("tensor")
    span = jnp.arange(blocks, dtype=jnp.int32) + tensor_pos * blocks
    onehot = (sketch_index[0][:, :, None] == span[None, None, :]).astype(jnp.bfloat16)
    local = jnp.einsum(
        "sij,sicd->sjcd", onehot, sketch_values[0], preferred_element_type=jnp.float32
    )
    local = local.astype(jnp.bfloat16).reshape(2, local_width, width)
    left_part = jnp.dot(acts[0], local[0], preferred_element_type=jnp.float32)
    right_part = jnp.dot(grads[0], local[1], preferred_element_type=jnp.float32)
    both = lax.psum(jnp.concatenate([left_part, right_part], axis=1), "tensor")
    left_all = both[:, :width].reshape(-1, TOK_EX, width)
    right_all = both[:, width:].reshape(-1, TOK_EX, width)
    outer = jnp.einsum("etk,etl->ekl", left_all, right_all, precision=lax.Precision.HIGHEST)
    current = outer.reshape(outer.shape[0], -1).T
    position = lax.axis_index("dp")
    for bit in range(lax.axis_size("dp").bit_length() - 1):
        partner = from_partner(current, "dp", bit)
        upper = jnp.right_shift(position, bit) % 2
        joined = jnp.where(
            upper == 0,
            jnp.concatenate([current, partner], axis=1),
            jnp.concatenate([partner, current], axis=1),
        )
        if joined.shape[1] <= RANK:
            current = joined
        else:
            current = reduce_plain(joined, layer_total)
    part_rows = current.shape[0] // tensor_count
    current = lax.dynamic_slice_in_dim(current, tensor_pos * part_rows, part_rows, 0)
    own_columns = current.shape[1] // lax.axis_size("dp")
    current = lax.dynamic_slice_in_dim(current, position * own_columns, own_columns, 1)
    return current


def solution(mesh):
    placed = (
        P("pipe", "dp", "tensor"),
        P("pipe", "dp", "tensor"),
        P("pipe", None, None),
        P("pipe", None, None, None, None),
    )
    return jax.shard_map(
        shards, mesh=mesh, in_specs=placed, out_specs=P(("pipe", "tensor"), "dp"), check_vma=False
    )
```

profile of v0, /device:TPU:1, one launch (start us, length us, event | category | flops | bytes accessed | tf_op | source)
XLA Modules:
  0.0 1064.1 jit_solution(16470218660606452282)
XLA Ops:
  10.4 48.4 %all-reduce.9.cloned.1.call-done = f32[512,64]{0,1:T(8,128)} async-done(((f32[512,64]{0,1:T(8,128)}), f32[512,64]{0,1:T(8,128)}) %all-reduce.9.cloned.1.call-update) | async-done | bytes 131088 | tf_op jit(solution)/shard_map/psum | solution.py:57
  60.0 4.8 fusion.84
  68.7 9.7 collective-permute-done
  82.8 20.0 %collective-permute-done.1 = f32[1024,256]{1,0:T(8,128)} collective-permute-done((f32[1024,256]{1,0:T(8,128)S(1)}, f32[1024,256]{1,0:T(8,128)}, u32[]{:S(2)}, u32[]{:S(2)}) %collective-permute-start.1) | collective-permute-done | bytes 1048608 | tf_op jit(solution)/shard_map/ppermute | solution.py:18
  109.0 114.7 %all-reduce.11.cloned.1.call-done = f32[256,256]{0,1:T(8,128)} async-done(((f32[256,256]{0,1:T(8,128)}), f32[256,256]{0,1:T(8,128)}) %all-reduce.11.cloned.1.call-update) | async-done | bytes 262160 | tf_op jit(solution)/shard_map/psum | solution.py:26
  226.5 11.7 %cholesky.214 = f32[128,128]{1,0:T(8,128)S(1)} custom-call(f32[128,128]{1,0:T(8,128)S(1)} %cholesky.346), custom_call_target="Cholesky" | custom-call | tf_op jit(solution)/shard_map/jit(cholesky)/cholesky | solution.py:30
  238.2 9.8 custom-call.16
  250.2 11.7 %cholesky.231 = f32[128,128]{1,0:T(8,128)S(1)} custom-call(f32[128,128]{1,0:T(8,128)S(1)} %convolution_subtract_fusion.3), custom_call_target="Cholesky" | custom-call | tf_op jit(solution)/shard_map/jit(cholesky)/cholesky | solution.py:30
  264.9 4.1 while.6
  269.6 20.5 %custom-call.17 = f32[2,128,128]{1,2,0:T(8,128)S(1)} custom-call(f32[2,128,128]{2,1,0:T(8,128)} %copy-done.18), custom_call_target="InvertDiagBlocksLowerTriangular" | custom-call | tf_op jit(solution)/shard_map/triangular_solve/custom-call.0 | solution.py:31
  292.5 4.3 fusion.10
  296.8 111.3 %all-reduce.13.cloned.1.call-done = f32[512,256]{1,0:T(8,128)} async-done(((f32[512,256]{1,0:T(8,128)}), f32[512,256]{1,0:T(8,128)}) %all-reduce.13.cloned.1.call-update) | async-done | bytes 524304 | tf_op jit(solution)/shard_map/psum | solution.py:26
  414.6 110.1 %all-reduce.15.cloned.1.call-done = f32[256,256]{0,1:T(8,128)} async-done(((f32[256,256]{0,1:T(8,128)}), f32[256,256]{0,1:T(8,128)}) %all-reduce.15.cloned.1.call-update) | async-done | bytes 262160 | tf_op jit(solution)/shard_map/psum | solution.py:26
  527.5 11.7 %cholesky.248 = f32[128,128]{1,0:T(8,128)S(1)} custom-call(f32[128,128]{1,0:T(8,128)S(1)} %cholesky.349), custom_call_target="Cholesky" | custom-call | tf_op jit(solution)/shard_map/jit(cholesky)/cholesky | solution.py:30
  539.3 9.8 custom-call.18
  551.3 11.7 %cholesky.265 = f32[128,128]{1,0:T(8,128)S(1)} custom-call(f32[128,128]{1,0:T(8,128)S(1)} %convolution_subtract_fusion.2), custom_call_target="Cholesky" | custom-call | tf_op jit(solution)/shard_map/jit(cholesky)/cholesky | solution.py:30
  566.5 4.1 while.7
  571.2 20.5 %custom-call.19 = f32[2,128,128]{1,2,0:T(8,128)S(1)} custom-call(f32[2,128,128]{2,1,0:T(8,128)} %copy-done.19), custom_call_target="InvertDiagBlocksLowerTriangular" | custom-call | tf_op jit(solution)/shard_map/triangular_solve/custom-call.0 | solution.py:31
  594.1 4.3 fusion.14
  598.4 111.3 %all-reduce.17.cloned.1.call-done = f32[512,256]{1,0:T(8,128)} async-done(((f32[512,256]{1,0:T(8,128)}), f32[512,256]{1,0:T(8,128)}) %all-reduce.17.cloned.1.call-update) | async-done | bytes 524304 | tf_op jit(solution)/shard_map/psum | solution.py:26
  709.7 3.5 fusion.88
  716.2 110.1 %all-reduce.19.cloned.1.call-done = f32[256,256]{0,1:T(8,128)} async-done(((f32[256,256]{0,1:T(8,128)}), f32[256,256]{0,1:T(8,128)}) %all-reduce.19.cloned.1.call-update) | async-done | bytes 262160 | tf_op jit(solution)/shard_map/psum | solution.py:26
  829.1 11.7 %cholesky.282 = f32[128,128]{1,0:T(8,128)S(1)} custom-call(f32[128,128]{1,0:T(8,128)S(1)} %cholesky.352), custom_call_target="Cholesky" | custom-call | tf_op jit(solution)/shard_map/jit(cholesky)/cholesky | solution.py:30
  840.9 9.8 custom-call.20
  852.9 11.7 %cholesky.299 = f32[128,128]{1,0:T(8,128)S(1)} custom-call(f32[128,128]{1,0:T(8,128)S(1)} %convolution_subtract_fusion.1), custom_call_target="Cholesky" | custom-call | tf_op jit(solution)/shard_map/jit(cholesky)/cholesky | solution.py:30
  868.1 3.9 while.8
  872.6 20.7 %custom-call.21 = f32[2,128,128]{1,2,0:T(8,128)S(1)} custom-call(f32[2,128,128]{2,1,0:T(8,128)} %copy-done.20), custom_call_target="InvertDiagBlocksLowerTriangular" | custom-call | tf_op jit(solution)/shard_map/triangular_solve/custom-call.0 | solution.py:31
  896.4 4.3 fusion.19
  900.8 111.3 %all-reduce.21.cloned.1.call-done = f32[512,256]{1,0:T(8,128)} async-done(((f32[512,256]{1,0:T(8,128)}), f32[512,256]{1,0:T(8,128)}) %all-reduce.21.cloned.1.call-update) | async-done | bytes 524304 | tf_op jit(solution)/shard_map/psum | solution.py:26
  1016.8 11.7 %cholesky.316 = f32[128,128]{1,0:T(8,128)S(1)} custom-call(f32[128,128]{1,0:T(8,128)S(1)} %cholesky.355), custom_call_target="Cholesky" | custom-call | tf_op jit(solution)/shard_map/jit(cholesky)/cholesky | solution.py:39
  1028.6 10.0 custom-call.22
  1040.7 11.7 %cholesky.333 = f32[128,128]{1,0:T(8,128)S(1)} custom-call(f32[128,128]{1,0:T(8,128)S(1)} %convolution_subtract_fusion), custom_call_target="Cholesky" | custom-call | tf_op jit(solution)/shard_map/jit(cholesky)/cholesky | solution.py:39
  (152 shorter events, 81.6 us)
Async XLA Ops:
  6.5 1.7 copy-start
  6.5 52.3 %all-reduce.9.cloned.1.call-start = ((), (), s32[]{:S(2)}) async-start(), calls=%async_computation | async-start | bytes 262144 | tf_op jit(solution)/shard_map/psum | solution.py:57
  6.5 2.4 copy-start.10
  10.4 213.3 %all-reduce.11.cloned.1.call-start = ((), (), s32[]{:S(2)}) async-start(), calls=%async_computation.1 | async-start | bytes 524288 | tf_op jit(solution)/shard_map/psum | solution.py:26
  67.5 1.3 copy-start.9
  67.5 10.9 %collective-permute-start = (f32[1024,128]{1,0:T(8,128)S(1)}, f32[1024,128]{1,0:T(8,128)}, u32[]{:S(2)}, u32[]{:S(2)}) collective-permute-start(f32[1024,128]{1,0:T(8,128)S(1)} %bitcast.167), channel_id=1, source_target_pairs={{0,4},{4,0},{8,12},{12,8},{1,5},{5,1},{9,13},{13,9},{2,6},{6,2},{1... | collective-permute-start | bytes 1572872 | tf_op jit(solution)/shard_map/ppermute | solution.py:18
  80.0 22.8 %collective-permute-start.1 = (f32[1024,256]{1,0:T(8,128)S(1)}, f32[1024,256]{1,0:T(8,128)}, u32[]{:S(2)}, u32[]{:S(2)}) collective-permute-start(f32[1024,256]{1,0:T(8,128)S(1)} %maximum_select_fusion.1), channel_id=1, source_target_pairs={{0,8},{8,0},{4,12},{12,4},{1,9},{9,1},{5,13},{13,5},{2,10},{10,2},... | collective-permute-start | bytes 3145736 | tf_op jit(solution)/shard_map/ppermute | solution.py:18
  104.8 1.4 copy-start.1
  108.8 299.3 %all-reduce.13.cloned.1.call-start = ((), (), s32[]{:S(2)}) async-start(), calls=%async_computation.2 | async-start | bytes 1048576 | tf_op jit(solution)/shard_map/psum | solution.py:26
  225.7 0.7 copy-start.15
  262.0 1.8 copy-start.11
  269.0 0.7 copy-start.18
  290.1 2.3 copy-start.2
  296.8 228.0 %all-reduce.15.cloned.1.call-start = ((), (), s32[]{:S(2)}) async-start(), calls=%async_computation.3 | async-start | bytes 524288 | tf_op jit(solution)/shard_map/psum | solution.py:26
  414.1 295.6 %all-reduce.17.cloned.1.call-start = ((), (), s32[]{:S(2)}) async-start(), calls=%async_computation.4 | async-start | bytes 1048576 | tf_op jit(solution)/shard_map/psum | solution.py:26
  526.8 0.7 copy-start.16
  563.0 2.5 copy-start.12
  570.6 0.7 copy-start.19
  591.7 2.3 copy-start.3
  598.4 227.9 %all-reduce.19.cloned.1.call-start = ((), (), s32[]{:S(2)}) async-start(), calls=%async_computation.5 | async-start | bytes 524288 | tf_op jit(solution)/shard_map/psum | solution.py:26
  715.7 296.4 %all-reduce.21.cloned.1.call-start = ((), (), s32[]{:S(2)}) async-start(), calls=%async_computation.6 | async-start | bytes 1048576 | tf_op jit(solution)/shard_map/psum | solution.py:26
  828.4 0.7 copy-start.17
  864.6 2.5 copy-start.13
  872.0 0.7 copy-start.20
  893.3 3.1 copy-start.4
  894.0 1.7 copy-start.5
  895.6 0.8 copy-start.7
  900.7 154.5 %copy-start.6 = (f32[128,1024]{1,0:T(8,128)S(1)}, f32[128,1024]{1,0:T(8,128)}, u32[]{:S(2)}) copy-start(f32[128,1024]{1,0:T(8,128)} %copy-done.5) | copy-start | bytes 1572868
  900.7 154.5 %copy-start.8 = (f32[1024,128]{0,1:T(8,128)S(1)}, f32[1024,128]{0,1:T(8,128)}, u32[]{:S(2)}) copy-start(f32[1024,128]{0,1:T(8,128)} %copy-done.7) | copy-start | bytes 1572868
  1016.1 0.7 copy-start.14
Sparse Core Ops, SparseCore 0:
  10.5 48.2 all-reduce.8
  108.9 114.7 all-reduce.10
  296.9 111.1 all-reduce.12
  414.3 110.4 all-reduce.14
  598.5 111.1 all-reduce.16
  715.8 110.4 all-reduce.18
  900.9 111.1 all-reduce.20
where the time goes:
time: 1070 us; the launch traced here: 1060 us
  waiting for transfers between devices  747 us (70%)
  other arithmetic  211 us (20%)
  matrix products  53.8 us (5%)
  local copies, waits for them, and re-layouts  27.5 us (3%)
  between operations  19.2 us (2%)
    psum x6, waiting for transfers between devices, layer_total(): return lax.psum(value, 'pipe')  669 us
    another operation x20, other arithmetic, orthonormal(): lower = jnp.linalg.cholesky(total(mm(block.T, block)))  103 us
    another operation x7, other arithmetic, orthonormal(): lax.linalg.triangular_solve(lower, block, left_side=False, lower=True, tr...  64.6 us
    psum x1, waiting for transfers between devices, shards(): both = lax.psum(jnp.concatenate([left_part, right_part], axis=1), 'tensor')  48.4 us
    another operation x7, other arithmetic, reduce_plain(): lower = jnp.linalg.cholesky(mm(weights.T, weights))  34.8 us
    dot_general x10, matrix products, mm(): return jnp.matmul(a, b, precision=lax.Precision.HIGHEST)  30.7 us
    ppermute x2, waiting for transfers between devices, from_partner(): return lax.ppermute(block, axis, route)  29.7 us
  transfers between devices with their start and end apart: 9, of which 9 were waited for; matrix products, arithmetic and copies ran while one was open for 0% of the time, Pallas kernels for 0%

commit v1 on v0

v1 whole, which is shorter than its diff:
```python
import jax
import jax.numpy as jnp
from jax import lax
from jax.sharding import PartitionSpec as P

RANK = 256
ITERS = 2
TOK_EX = 4


def mm(a, b):
    return jnp.matmul(a, b, precision=lax.Precision.HIGHEST)


def mm_tn(a, b):
    return lax.dot_general(a, b, (((0,), (0,)), ((), ())), precision=lax.Precision.HIGHEST)


def solve_lower_t(lower, block):
    return lax.linalg.triangular_solve(lower, block, left_side=False, lower=True, transpose_a=True)


def merged_coords(gram):
    cols = gram.shape[0]
    eye = jnp.eye(RANK, dtype=gram.dtype)
    pick = jnp.concatenate([eye] * (cols // RANK), axis=0)
    lower = jnp.linalg.cholesky(mm_tn(pick, mm(gram, pick)))
    coords = solve_lower_t(lower, pick)
    for turn in range(ITERS):
        image = mm(gram, coords)
        lower = jnp.linalg.cholesky(mm_tn(image, mm(gram, image)))
        coords = solve_lower_t(lower, image)
    weights = mm(gram, coords)
    lower = jnp.linalg.cholesky(mm_tn(weights, weights))
    return mm(coords, lower)


def shards(acts, grads, sketch_index, sketch_values):
    local_width = acts.shape[2]
    blocks = local_width // 128
    width = sketch_values.shape[4]
    tensor_pos = lax.axis_index("tensor")
    tensor_count = lax.axis_size("tensor")
    dp_pos = lax.axis_index("dp")
    dp_count = lax.axis_size("dp")
    span = jnp.arange(blocks, dtype=jnp.int32) + tensor_pos * blocks
    onehot = (sketch_index[0][:, :, None] == span[None, None, :]).astype(jnp.bfloat16)
    local = jnp.einsum(
        "sij,sicd->sjcd", onehot, sketch_values[0], preferred_element_type=jnp.float32
    )
    local = local.astype(jnp.bfloat16).reshape(2, local_width, width)
    left_part = jnp.dot(acts[0], local[0], preferred_element_type=jnp.float32)
    right_part = jnp.dot(grads[0], local[1], preferred_element_type=jnp.float32)
    both = lax.psum(jnp.concatenate([left_part, right_part], axis=1), "tensor")
    both = lax.all_gather(both, "dp", axis=0, tiled=True)
    left_all = both[:, :width].reshape(-1, TOK_EX, width)
    right_all = both[:, width:].reshape(-1, TOK_EX, width)
    outer = jnp.einsum("etk,etl->ekl", left_all, right_all, precision=lax.Precision.HIGHEST)
    joined_t = outer.reshape(outer.shape[0], -1)
    gram = lax.psum(mm(joined_t, joined_t.T), "pipe")
    coords = merged_coords(gram)
    part_rows = joined_t.shape[1] // tensor_count
    rows = lax.dynamic_slice_in_dim(joined_t, tensor_pos * part_rows, part_rows, 1)
    own_columns = coords.shape[1] // dp_count
    coords = lax.dynamic_slice_in_dim(coords, dp_pos * own_columns, own_columns, 1)
    return mm_tn(rows, coords)


def solution(mesh):
    placed = (
        P("pipe", "dp", "tensor"),
        P("pipe", "dp", "tensor"),
        P("pipe", None, None),
        P("pipe", None, None, None, None),
    )
    return jax.shard_map(
        shards, mesh=mesh, in_specs=placed, out_specs=P(("pipe", "tensor"), "dp"), check_vma=False
    )
```

time: 1070 us -> 496 us (0.46)
  waiting for transfers between devices: 747 us -> 165 us
    psum x6 -> x1, waiting for transfers between devices: 669 us -> 116 us  [shards(): gram = lax.psum(mm(joined_t, joined_t.T), 'pipe')]
    ppermute x2 -> x0, waiting for transfers between devices: 29.7 us -> none  [from_partner(): return lax.ppermute(block, axis, route)]
    dot_general x10 -> x8, matrix products: 30.7 us -> 14.7 us  [mm(): return jnp.matmul(a, b, precision=lax.Precision.HIGHEST)]
    dot_general x1, matrix products: 4.81 us -> 16.5 us  [shards(): jnp.einsum('etk,etl->ekl', left_all, right_all, precision=lax.Precision.H...]
  transfers between devices with their start and end apart: 9 -> 2, of which waited for: 9 -> 2; matrix products, arithmetic and copies ran while one was open for 0% -> 0% of each run, Pallas kernels for 0% -> 0%
where the time goes in v1:
time: 496 us; the launch traced here: 488 us
  other arithmetic  207 us (42%)
  waiting for transfers between devices  165 us (33%)
  matrix products  57 us (11%)
  local copies, waits for them, and re-layouts  29.2 us (6%)
  between operations  19.3 us (4%)
  blocking collectives  10.5 us (2%)
    psum x1, waiting for transfers between devices, shards(): gram = lax.psum(mm(joined_t, joined_t.T), 'pipe')  116 us
    another operation x14, other arithmetic, merged_coords(): lower = jnp.linalg.cholesky(mm_tn(image, mm(gram, image)))  69.8 us
    another operation x7, other arithmetic, solve_lower_t(): lax.linalg.triangular_solve(lower, block, left_side=False, lower=True, tr...  64.4 us
    psum x1, waiting for transfers between devices, shards(): both = lax.psum(jnp.concatenate([left_part, right_part], axis=1), 'tensor')  48.4 us
    another operation x7, other arithmetic, merged_coords(): lower = jnp.linalg.cholesky(mm_tn(weights, weights))  34.8 us
    another operation x6, other arithmetic, merged_coords(): lower = jnp.linalg.cholesky(mm_tn(pick, mm(gram, pick)))  34.4 us
    dot_general x1, matrix products, shards(): jnp.einsum('etk,etl->ekl', left_all, right_all, precision=lax.Precision.H...  16.5 us
    dot_general x8, matrix products, mm(): return jnp.matmul(a, b, precision=lax.Precision.HIGHEST)  14.7 us
  transfers between devices with their start and end apart: 2, of which 2 were waited for; matrix products, arithmetic and copies ran while one was open for 0% of the time, Pallas kernels for 0%

profile of v1, /device:TPU:1, one launch (start us, length us, event | category | flops | bytes accessed | tf_op | source)
XLA Modules:
  0.0 487.8 jit_solution(8322790528402684456)
XLA Ops:
  10.4 48.4 %all-reduce.4.cloned.1.call-done = f32[512,64]{0,1:T(8,128)} async-done(((f32[512,64]{0,1:T(8,128)}), f32[512,64]{0,1:T(8,128)}) %all-reduce.4.cloned.1.call-update) | async-done | bytes 131088 | tf_op jit(solution)/shard_map/psum | solution.py:54
  58.8 10.5 %all_gather.3 = f32[2048,64]{0,1:T(8,128)S(1)} all-gather(f32[512,64]{0,1:T(8,128)} %all-reduce.4.cloned.1.call-done), channel_id=1, replica_groups=mesh['pipe'=16,'dp'=4,'tensor'=4] {'dp'}, dimensions={0}, use_global_device_ids=true | all-gather | bytes 655360 | tf_op jit(solution)/shard_map/all_gather | solution.py:55
  72.8 16.5 %fusion.90 = f32[512,32,32]{2,1,0:T(8,128)} fusion(f32[512,4,32]{2,1,0:T(4,128)S(1)} %bitcast.168, f32[512,4,32]{2,1,0:T(4,128)} %bitcast.169), kind=kOutput, calls=%fused_computation.147 | convolution fusion | flops 25165824 | bytes 2621440 | tf_op jit(solution)/shard_map/etk,etl->ekl/dot_general | solution.py:58
  89.2 6.4 %copy.17 = f32[512,32,32]{0,2,1:T(8,128)} copy(f32[512,32,32]{2,1,0:T(8,128)} %fusion.90) | data formatting | bytes 4194304 | tf_op jit(solution)/shard_map/etk,etl->ekl/dot_general | solution.py:58
  95.7 6.8 %convolution_bitcast_fusion = f32[512,512]{1,0:T(8,128)} fusion(f32[512,32,32]{0,2,1:T(8,128)} %copy.17), kind=kOutput, calls=%fused_computation.10 | convolution fusion | flops 3221225472 | bytes 3145728 | tf_op jit(solution)/shard_map/dot_general | solution.py:12
  103.4 116.2 %all-reduce.6.cloned.1.call-done = f32[512,512]{1,0:T(8,128)} async-done(((f32[512,512]{1,0:T(8,128)}), f32[512,512]{1,0:T(8,128)}) %all-reduce.6.cloned.1.call-update) | async-done | bytes 1048592 | tf_op jit(solution)/shard_map/psum | solution.py:60
  219.6 1.8 fusion.70
  223.0 11.7 %cholesky.214 = f32[128,128]{1,0:T(8,128)S(1)} custom-call(f32[128,128]{1,0:T(8,128)S(1)} %cholesky.346), custom_call_target="Cholesky" | custom-call | tf_op jit(solution)/shard_map/jit(cholesky)/cholesky | solution.py:27
  234.7 9.8 %custom-call.16 = f32[1,128,128]{1,2,0:T(8,128)S(1)} custom-call(f32[1,128,128]{2,1,0:T(8,128)S(1)} %get-tuple-element.79), custom_call_target="InvertDiagBlocksLowerTriangular" | custom-call | tf_op jit(solution)/shard_map/jit(cholesky)/cholesky | solution.py:27
  246.8 12.1 %cholesky.231 = f32[128,128]{1,0:T(8,128)S(1)} custom-call(f32[128,128]{1,0:T(8,128)S(1)} %convolution_subtract_fusion.6), custom_call_target="Cholesky" | custom-call | tf_op jit(solution)/shard_map/jit(cholesky)/cholesky | solution.py:27
  262.0 4.1 while.6
  266.7 20.5 %custom-call.17 = f32[2,128,128]{1,2,0:T(8,128)S(1)} custom-call(f32[2,128,128]{2,1,0:T(8,128)} %copy-done.14), custom_call_target="InvertDiagBlocksLowerTriangular" | custom-call | tf_op jit(solution)/shard_map/triangular_solve/custom-call.0 | solution.py:20
  288.6 1.5 convolution_subtract_fusion.2
  296.2 11.7 %cholesky.248 = f32[128,128]{1,0:T(8,128)S(1)} custom-call(f32[128,128]{1,0:T(8,128)S(1)} %cholesky.349), custom_call_target="Cholesky" | custom-call | tf_op jit(solution)/shard_map/jit(cholesky)/cholesky | solution.py:31
  307.9 9.8 %custom-call.18 = f32[1,128,128]{1,2,0:T(8,128)S(1)} custom-call(f32[1,128,128]{2,1,0:T(8,128)S(1)} %get-tuple-element.75), custom_call_target="InvertDiagBlocksLowerTriangular" | custom-call | tf_op jit(solution)/shard_map/jit(cholesky)/cholesky | solution.py:31
  319.9 11.9 %cholesky.265 = f32[128,128]{1,0:T(8,128)S(1)} custom-call(f32[128,128]{1,0:T(8,128)S(1)} %convolution_subtract_fusion.5), custom_call_target="Cholesky" | custom-call | tf_op jit(solution)/shard_map/jit(cholesky)/cholesky | solution.py:31
  335.4 4.1 while.7
  336.1 1.4 bitcast_dynamic-update-slice_fusion.7
  338.1 1.4 bitcast_dynamic-update-slice_fusion.7
  340.2 20.5 %custom-call.19 = f32[2,128,128]{1,2,0:T(8,128)S(1)} custom-call(f32[2,128,128]{2,1,0:T(8,128)} %copy-done.15), custom_call_target="InvertDiagBlocksLowerTriangular" | custom-call | tf_op jit(solution)/shard_map/triangular_solve/custom-call.0 | solution.py:20
  362.1 1.5 convolution_subtract_fusion.1
  369.6 11.7 %cholesky.282 = f32[128,128]{1,0:T(8,128)S(1)} custom-call(f32[128,128]{1,0:T(8,128)S(1)} %cholesky.352), custom_call_target="Cholesky" | custom-call | tf_op jit(solution)/shard_map/jit(cholesky)/cholesky | solution.py:31
  381.4 9.8 %custom-call.20 = f32[1,128,128]{1,2,0:T(8,128)S(1)} custom-call(f32[1,128,128]{2,1,0:T(8,128)S(1)} %get-tuple-element.71), custom_call_target="InvertDiagBlocksLowerTriangular" | custom-call | tf_op jit(solution)/shard_map/jit(cholesky)/cholesky | solution.py:31
  393.4 12.1 %cholesky.299 = f32[128,128]{1,0:T(8,128)S(1)} custom-call(f32[128,128]{1,0:T(8,128)S(1)} %convolution_subtract_fusion.4), custom_call_target="Cholesky" | custom-call | tf_op jit(solution)/shard_map/jit(cholesky)/cholesky | solution.py:31
  409.2 4.1 while.8
  409.8 1.4 bitcast_dynamic-update-slice_fusion.8
  414.6 20.5 %custom-call.21 = f32[2,128,128]{1,2,0:T(8,128)S(1)} custom-call(f32[2,128,128]{2,1,0:T(8,128)} %copy-done.16), custom_call_target="InvertDiagBlocksLowerTriangular" | custom-call | tf_op jit(solution)/shard_map/triangular_solve/custom-call.0 | solution.py:20
  436.5 1.6 convolution_subtract_fusion
  440.8 11.7 %cholesky.316 = f32[128,128]{1,0:T(8,128)S(1)} custom-call(f32[128,128]{1,0:T(8,128)S(1)} %cholesky.355), custom_call_target="Cholesky" | custom-call | tf_op jit(solution)/shard_map/jit(cholesky)/cholesky | solution.py:34
  452.6 9.8 %custom-call.22 = f32[1,128,128]{1,2,0:T(8,128)S(1)} custom-call(f32[1,128,128]{2,1,0:T(8,128)S(1)} %get-tuple-element.67), custom_call_target="InvertDiagBlocksLowerTriangular" | custom-call | tf_op jit(solution)/shard_map/jit(cholesky)/cholesky | solution.py:34
  462.9 11.9 %cholesky.333 = f32[128,128]{1,0:T(8,128)S(1)} custom-call(f32[128,128]{1,0:T(8,128)S(1)} %convolution_subtract_fusion.3), custom_call_target="Cholesky" | custom-call | tf_op jit(solution)/shard_map/jit(cholesky)/cholesky | solution.py:34
  478.4 2.4 fusion.18
  (127 shorter events, 54.9 us)
Async XLA Ops:
  6.5 1.7 copy-start
  6.5 52.3 %all-reduce.4.cloned.1.call-start = ((), (), s32[]{:S(2)}) async-start(), calls=%async_computation | async-start | bytes 262144 | tf_op jit(solution)/shard_map/psum | solution.py:54
  6.5 2.4 copy-start.6
  10.4 209.2 %all-reduce.6.cloned.1.call-start = ((), (), s32[]{:S(2)}) async-start(), calls=%async_computation.1 | async-start | bytes 2097152 | tf_op jit(solution)/shard_map/psum | solution.py:60
  222.3 0.7 copy-start.11
  244.6 46.0 %copy-start.1 = (f32[512,512]{1,0:T(8,128)S(1)}, f32[512,512]{1,0:T(8,128)}, u32[]{:S(2)}) copy-start(f32[512,512]{1,0:T(8,128)} %all-reduce.6.cloned.1.call-done) | copy-start | bytes 3145732
  259.0 1.9 copy-start.10
  266.1 0.6 copy-start.14
  291.6 1.0 copy-start.3
  295.4 0.7 copy-start.12
  331.8 2.6 copy-start.8
  339.6 0.7 copy-start.15
  365.1 1.0 copy-start.2
  368.9 0.7 copy-start.13
  405.5 2.6 copy-start.9
  413.3 0.7 copy-start.16
  413.9 0.7 copy-start.7
  438.5 1.0 copy-start.4
  440.6 36.8 %copy-start.5 = (f32[512,128]{0,1:T(8,128)S(1)}, f32[512,128]{0,1:T(8,128)}, u32[]{:S(2)}) copy-start(f32[512,128]{0,1:T(8,128)} %copy-done.4) | copy-start | bytes 786436
Sparse Core Ops, SparseCore 0:
  10.5 48.2 all-reduce.3
  102.6 116.9 all-reduce.5

commit v2 on v1

--- a/solution.py
+++ b/solution.py
@@ -14,6 +14,40 @@
 
 def mm_tn(a, b):
     return lax.dot_general(a, b, (((0,), (0,)), ((), ())), precision=lax.Precision.HIGHEST)
+
+
+def exchange(block, axis, bit):
+    count = lax.axis_size(axis)
+    return lax.ppermute(block, axis, [(i, i ^ (1 << bit)) for i in range(count)])
+
+
+def butterfly_sum(block, axis):
+    for bit in range(lax.axis_size(axis).bit_length() - 1):
+        block = block + exchange(block, axis, bit)
+    return block
+
+
+def halving_doubling_sum(block, axis):
+    position = lax.axis_index(axis)
+    bits = lax.axis_size(axis).bit_length() - 1
+    for bit in range(bits):
+        half = block.shape[0] // 2
+        upper = jnp.right_shift(position, bit) % 2 == 1
+        keep = jnp.where(upper, block[half:], block[:half])
+        give = jnp.where(upper, block[:half], block[half:])
+        block = keep + exchange(give, axis, bit)
+    return doubling_gather(block, axis, reversed(range(bits)))
+
+
+def doubling_gather(block, axis, bits):
+    position = lax.axis_index(axis)
+    for bit in bits:
+        upper = jnp.right_shift(position, bit) % 2 == 1
+        other = exchange(block, axis, bit)
+        block = jnp.where(
+            upper, jnp.concatenate([other, block], 0), jnp.concatenate([block, other], 0)
+        )
+    return block
 
 
 def solve_lower_t(lower, block):
@@ -51,13 +85,14 @@
     local = local.astype(jnp.bfloat16).reshape(2, local_width, width)
     left_part = jnp.dot(acts[0], local[0], preferred_element_type=jnp.float32)
     right_part = jnp.dot(grads[0], local[1], preferred_element_type=jnp.float32)
-    both = lax.psum(jnp.concatenate([left_part, right_part], axis=1), "tensor")
-    both = lax.all_gather(both, "dp", axis=0, tiled=True)
+    both = butterfly_sum(jnp.concatenate([left_part, right_part], axis=1), "tensor")
+    dp_bits = dp_count.bit_length() - 1
+    both = doubling_gather(both, "dp", range(dp_bits))
     left_all = both[:, :width].reshape(-1, TOK_EX, width)
     right_all = both[:, width:].reshape(-1, TOK_EX, width)
     outer = jnp.einsum("etk,etl->ekl", left_all, right_all, precision=lax.Precision.HIGHEST)
     joined_t = outer.reshape(outer.shape[0], -1)
-    gram = lax.psum(mm(joined_t, joined_t.T), "pipe")
+    gram = halving_doubling_sum(mm(joined_t, joined_t.T), "pipe")
     coords = merged_coords(gram)
     part_rows = joined_t.shape[1] // tensor_count
     rows = lax.dynamic_slice_in_dim(joined_t, tensor_pos * part_rows, part_rows, 1)

time: 496 us -> 367 us (0.74)
  waiting for transfers between devices: 165 us -> 45.4 us
  starting transfers between devices: 0.04 us -> 34.7 us
  between operations: 19.3 us -> 6.15 us
  blocking collectives: 10.5 us -> 0 us
  other arithmetic: 207 us -> 201 us
  matrix products: 57 us -> 51.7 us
    psum x2 -> x0, waiting for transfers between devices: 165 us -> none  [the longest x1 116 us: shards(): gram = lax.psum(mm(joined_t, joined_t.T), 'pipe')]
    ppermute x0 -> x12, waiting for transfers between devices: none -> 45.4 us  [exchange(): return lax.ppermute(block, axis, [(i, i ^ 1 << bit) for i in range(count)])]
    ppermute x0 -> x12, starting transfers between devices: none -> 34.7 us  [exchange(): return lax.ppermute(block, axis, [(i, i ^ 1 << bit) for i in range(count)])]
    all_gather x1 -> x0, blocking collectives: 10.5 us -> none  [shards(): both = lax.all_gather(both, 'dp', axis=0, tiled=True)]
    another operation x9, matrix products: 10 us -> 4.27 us  [solve_lower_t(): lax.linalg.triangular_solve(lower, block, left_side=False, lower=True, tr...]
    dot_general x8, matrix products: 14.7 us -> 20.3 us  [mm(): return jnp.matmul(a, b, precision=lax.Precision.HIGHEST)]
  transfers between devices with their start and end apart: 2 -> 12, of which waited for: 2 -> 12; matrix products, arithmetic and copies ran while one was open for 0% -> 0% of each run, Pallas kernels for 0% -> 0%
where the time goes in v2:
time: 367 us; the launch traced here: 364 us
  other arithmetic  201 us (55%)
  matrix products  51.7 us (14%)
  waiting for transfers between devices  45.4 us (12%)
  starting transfers between devices  34.7 us (9%)
  local copies, waits for them, and re-layouts  24.5 us (7%)
  between operations  6.15 us (2%)
    another operation x14, other arithmetic, merged_coords(): lower = jnp.linalg.cholesky(mm_tn(image, mm(gram, image)))  69.9 us
    another operation x7, other arithmetic, solve_lower_t(): lax.linalg.triangular_solve(lower, block, left_side=False, lower=True, tr...  60.3 us
    ppermute x12, waiting for transfers between devices, exchange(): return lax.ppermute(block, axis, [(i, i ^ 1 << bit) for i in range(count)])  45.4 us
    another operation x7, other arithmetic, merged_coords(): lower = jnp.linalg.cholesky(mm_tn(weights, weights))  34.8 us
    ppermute x12, starting transfers between devices, exchange(): return lax.ppermute(block, axis, [(i, i ^ 1 << bit) for i in range(count)])  34.7 us
    another operation x6, other arithmetic, merged_coords(): lower = jnp.linalg.cholesky(mm_tn(pick, mm(gram, pick)))  34 us
    dot_general x8, matrix products, mm(): return jnp.matmul(a, b, precision=lax.Precision.HIGHEST)  20.3 us
    dot_general x1, matrix products, shards(): jnp.einsum('etk,etl->ekl', left_all, right_all, precision=lax.Precision.H...  16.5 us
  transfers between devices with their start and end apart: 12, of which 12 were waited for; matrix products, arithmetic and copies ran while one was open for 0% of the time, Pallas kernels for 0%

profile of v2, /device:TPU:1, one launch (start us, length us, event | category | flops | bytes accessed | tf_op | source)
XLA Modules:
  0.0 363.5 jit_solution(3316798447976136950)
XLA Ops:
  7.8 3.7 %collective-permute-start.1 = (f32[512,64]{0,1:T(8,128)S(1)}, f32[512,64]{0,1:T(8,128)S(1)}, u32[]{:S(2)}, u32[]{:S(2)}) collective-permute-start(f32[512,64]{0,1:T(8,128)S(1)} %fusion.87), channel_id=1, source_target_pairs={{0,2},{1,3},{2,0},{3,1},{4,6},{5,7},{6,4},{7,5},{8,10},{9,11},{10,... | collective-permute-start | bytes 393224 | tf_op jit(solution)/shard_map/ppermute | solution.py:21
  17.8 3.4 collective-permute-start.3
  21.2 4.8 %collective-permute-done.3 = f32[1024,64]{0,1:T(8,128)S(1)} collective-permute-done((f32[1024,64]{0,1:T(8,128)S(1)}, f32[1024,64]{0,1:T(8,128)S(1)}, u32[]{:S(2)}, u32[]{:S(2)}) %collective-permute-start.3) | collective-permute-done | bytes 262176 | tf_op jit(solution)/shard_map/ppermute | solution.py:21
  29.4 16.5 %fusion.95 = f32[512,32,32]{2,1,0:T(8,128)} fusion(f32[512,4,32]{2,1,0:T(4,128)S(1)} %bitcast.160, f32[512,4,32]{2,1,0:T(4,128)} %bitcast.161), kind=kOutput, calls=%fused_computation.166 | convolution fusion | flops 25165824 | bytes 2621440 | tf_op jit(solution)/shard_map/etk,etl->ekl/dot_general | solution.py:93
  45.9 6.3 %copy.17 = f32[512,32,32]{0,2,1:T(8,128)} copy(f32[512,32,32]{2,1,0:T(8,128)} %fusion.95) | data formatting | bytes 4194304 | tf_op jit(solution)/shard_map/etk,etl->ekl/dot_general | solution.py:93
  52.2 5.8 %convolution_bitcast_fusion = f32[512,512]{1,0:T(8,128)S(1)} fusion(f32[512,32,32]{0,2,1:T(8,128)} %copy.17), kind=kOutput, calls=%fused_computation.10 | convolution fusion | flops 3221225472 | bytes 3145728 | tf_op jit(solution)/shard_map/dot_general | solution.py:12
  59.0 5.9 %collective-permute-start.4 = (f32[256,512]{1,0:T(8,128)S(1)}, f32[256,512]{1,0:T(8,128)S(1)}, u32[]{:S(2)}, u32[]{:S(2)}) collective-permute-start(f32[256,512]{1,0:T(8,128)S(1)} %slice_select_fusion), channel_id=1, source_target_pairs={{0,16},{16,0},{32,48},{48,32},{64,80},{80,64},{96,112},{112,96},{1... | collective-permute-start | bytes 1572872 | tf_op jit(solution)/shard_map/ppermute | solution.py:21
  68.1 7.3 %collective-permute-done.5 = f32[128,512]{1,0:T(8,128)S(1)} collective-permute-done((f32[128,512]{1,0:T(8,128)S(1)}, f32[128,512]{1,0:T(8,128)S(1)}, u32[]{:S(2)}, u32[]{:S(2)}) %collective-permute-start.5) | collective-permute-done | bytes 262176 | tf_op jit(solution)/shard_map/ppermute | solution.py:21
  77.5 6.7 %collective-permute-done.6 = f32[64,512]{1,0:T(8,128)S(1)} collective-permute-done((f32[64,512]{1,0:T(8,128)S(1)}, f32[64,512]{1,0:T(8,128)S(1)}, u32[]{:S(2)}, u32[]{:S(2)}) %collective-permute-start.6) | collective-permute-done | bytes 131104 | tf_op jit(solution)/shard_map/ppermute | solution.py:21
  84.2 5.7 %collective-permute-start.7 = (f32[32,512]{1,0:T(8,128)S(1)}, f32[32,512]{1,0:T(8,128)S(1)}, u32[]{:S(2)}, u32[]{:S(2)}) collective-permute-start(f32[32,512]{1,0:T(8,128)S(1)} %slice_select_fusion.3), channel_id=1, source_target_pairs={{0,128},{16,144},{32,160},{48,176},{64,192},{80,208},{96,224},{112... | collective-permute-start | bytes 196616 | tf_op jit(solution)/shard_map/ppermute | solution.py:21
  91.5 5.5 %collective-permute-start.8 = (f32[32,512]{1,0:T(8,128)S(1)}, f32[32,512]{1,0:T(8,128)S(1)}, u32[]{:S(2)}, u32[]{:S(2)}) collective-permute-start(f32[32,512]{1,0:T(8,128)S(1)} %select_add_fusion.3), channel_id=1, source_target_pairs={{0,128},{16,144},{32,160},{48,176},{64,192},{80,208},{96,224},{112... | collective-permute-start | bytes 196616 | tf_op jit(solution)/shard_map/ppermute | solution.py:21
  98.9 6.8 %collective-permute-done.9 = f32[64,512]{1,0:T(8,128)S(1)} collective-permute-done((f32[64,512]{1,0:T(8,128)S(1)}, f32[64,512]{1,0:T(8,128)S(1)}, u32[]{:S(2)}, u32[]{:S(2)}) %collective-permute-start.9) | collective-permute-done | bytes 131104 | tf_op jit(solution)/shard_map/ppermute | solution.py:21
  105.8 6.0 %collective-permute-done.10 = f32[128,512]{1,0:T(8,128)S(1)} collective-permute-done((f32[128,512]{1,0:T(8,128)S(1)}, f32[128,512]{1,0:T(8,128)S(1)}, u32[]{:S(2)}, u32[]{:S(2)}) %collective-permute-start.10) | collective-permute-done | bytes 262176 | tf_op jit(solution)/shard_map/ppermute | solution.py:21
  111.9 4.5 %collective-permute-start.11 = (f32[256,512]{1,0:T(8,128)S(1)}, f32[256,512]{1,0:T(8,128)}, u32[]{:S(2)}, u32[]{:S(2)}) collective-permute-start(f32[256,512]{1,0:T(8,128)S(1)} %maximum_select_fusion.2), channel_id=1, source_target_pairs={{0,16},{16,0},{32,48},{48,32},{64,80},{80,64},{96,112},{112,96},{1... | collective-permute-start | bytes 1572872 | tf_op jit(solution)/shard_map/ppermute | solution.py:21
  120.8 11.7 %cholesky.214 = f32[128,128]{1,0:T(8,128)S(1)} custom-call(f32[128,128]{1,0:T(8,128)S(1)} %cholesky.346), custom_call_target="Cholesky" | custom-call | tf_op jit(solution)/shard_map/jit(cholesky)/cholesky | solution.py:61
  132.5 9.8 %custom-call.16 = f32[1,128,128]{1,2,0:T(8,128)S(1)} custom-call(f32[1,128,128]{2,1,0:T(8,128)S(1)} %get-tuple-element.79), custom_call_target="InvertDiagBlocksLowerTriangular" | custom-call | tf_op jit(solution)/shard_map/jit(cholesky)/cholesky | solution.py:61
  142.8 11.7 %cholesky.231 = f32[128,128]{1,0:T(8,128)S(1)} custom-call(f32[128,128]{1,0:T(8,128)S(1)} %convolution_subtract_fusion.4), custom_call_target="Cholesky" | custom-call | tf_op jit(solution)/shard_map/jit(cholesky)/cholesky | solution.py:61
  156.7 4.1 %while.6 = (s32[]{:T(128)}, f32[256,256]{1,0:T(8,128)S(1)}, s32[2,2]{1,0:T(2,128)S(1)}, f32[2,128,128]{2,1,0:T(8,128)S(1)}, s32[]{:T(128)}) while((s32[]{:T(128)}, f32[256,256]{1,0:T(8,128)S(1)}, s32[2,2]{1,0:T(2,128)S(1)}, f32[2,128,128]{2,1,0:T(8,128)S(1)}, s32[]{:T(128)}) %tuple.65), condition=%wide.while_cond, body=%wide.while_body.sunk | while | flops 2 | bytes 131181 | solution.py:54
  161.4 20.9 %custom-call.17 = f32[2,128,128]{1,2,0:T(8,128)S(1)} custom-call(f32[2,128,128]{2,1,0:T(8,128)} %copy-done.6), custom_call_target="InvertDiagBlocksLowerTriangular" | custom-call | tf_op jit(solution)/shard_map/triangular_solve/custom-call.0 | solution.py:54
  189.4 11.7 %cholesky.248 = f32[128,128]{1,0:T(8,128)S(1)} custom-call(f32[128,128]{1,0:T(8,128)S(1)} %cholesky.349), custom_call_target="Cholesky" | custom-call | tf_op jit(solution)/shard_map/jit(cholesky)/cholesky | solution.py:65
  201.2 9.8 %custom-call.18 = f32[1,128,128]{1,2,0:T(8,128)S(1)} custom-call(f32[1,128,128]{2,1,0:T(8,128)S(1)} %get-tuple-element.75), custom_call_target="InvertDiagBlocksLowerTriangular" | custom-call | tf_op jit(solution)/shard_map/jit(cholesky)/cholesky | solution.py:65
  211.5 11.9 %cholesky.265 = f32[128,128]{1,0:T(8,128)S(1)} custom-call(f32[128,128]{1,0:T(8,128)S(1)} %convolution_subtract_fusion.3), custom_call_target="Cholesky" | custom-call | tf_op jit(solution)/shard_map/jit(cholesky)/cholesky | solution.py:65
  226.1 4.1 %while.7 = (s32[]{:T(128)}, f32[256,256]{1,0:T(8,128)S(1)}, s32[2,2]{1,0:T(2,128)S(1)}, f32[2,128,128]{2,1,0:T(8,128)S(1)}, s32[]{:T(128)}) while((s32[]{:T(128)}, f32[256,256]{1,0:T(8,128)S(1)}, s32[2,2]{1,0:T(2,128)S(1)}, f32[2,128,128]{2,1,0:T(8,128)S(1)}, s32[]{:T(128)}) %tuple.74), condition=%wide.while_cond.clone, body=%wide.while_body.clone.sunk | while | flops 2 | bytes 131181 | solution.py:54
  230.2 19.7 %custom-call.19 = f32[2,128,128]{1,2,0:T(8,128)S(1)} custom-call(f32[2,128,128]{2,1,0:T(8,128)S(1)} %get-tuple-element.28), custom_call_target="InvertDiagBlocksLowerTriangular" | custom-call | tf_op jit(solution)/shard_map/triangular_solve/custom-call.0 | solution.py:54
  257.3 11.7 %cholesky.282 = f32[128,128]{1,0:T(8,128)S(1)} custom-call(f32[128,128]{1,0:T(8,128)S(1)} %cholesky.352), custom_call_target="Cholesky" | custom-call | tf_op jit(solution)/shard_map/jit(cholesky)/cholesky | solution.py:65
  269.1 9.8 %custom-call.20 = f32[1,128,128]{1,2,0:T(8,128)S(1)} custom-call(f32[1,128,128]{2,1,0:T(8,128)S(1)} %get-tuple-element.71), custom_call_target="InvertDiagBlocksLowerTriangular" | custom-call | tf_op jit(solution)/shard_map/jit(cholesky)/cholesky | solution.py:65
  279.4 12.1 %cholesky.299 = f32[128,128]{1,0:T(8,128)S(1)} custom-call(f32[128,128]{1,0:T(8,128)S(1)} %convolution_subtract_fusion.2), custom_call_target="Cholesky" | custom-call | tf_op jit(solution)/shard_map/jit(cholesky)/cholesky | solution.py:65
  294.3 4.1 %while.8 = (s32[]{:T(128)}, f32[256,256]{1,0:T(8,128)S(1)}, s32[2,2]{1,0:T(2,128)S(1)}, f32[2,128,128]{2,1,0:T(8,128)S(1)}, s32[]{:T(128)}) while((s32[]{:T(128)}, f32[256,256]{1,0:T(8,128)S(1)}, s32[2,2]{1,0:T(2,128)S(1)}, f32[2,128,128]{2,1,0:T(8,128)S(1)}, s32[]{:T(128)}) %tuple.75), condition=%wide.while_cond.clone.1, body=%wide.while_body.clone.1.sunk | while | flops 2 | bytes 131181 | solution.py:54
  298.4 19.7 %custom-call.21 = f32[2,128,128]{1,2,0:T(8,128)S(1)} custom-call(f32[2,128,128]{2,1,0:T(8,128)S(1)} %get-tuple-element.29), custom_call_target="InvertDiagBlocksLowerTriangular" | custom-call | tf_op jit(solution)/shard_map/triangular_solve/custom-call.0 | solution.py:54
  323.3 11.7 %cholesky.316 = f32[128,128]{1,0:T(8,128)S(1)} custom-call(f32[128,128]{1,0:T(8,128)S(1)} %cholesky.355), custom_call_target="Cholesky" | custom-call | tf_op jit(solution)/shard_map/jit(cholesky)/cholesky | solution.py:68
  335.1 9.8 %custom-call.22 = f32[1,128,128]{1,2,0:T(8,128)S(1)} custom-call(f32[1,128,128]{2,1,0:T(8,128)S(1)} %get-tuple-element.67), custom_call_target="InvertDiagBlocksLowerTriangular" | custom-call | tf_op jit(solution)/shard_map/jit(cholesky)/cholesky | solution.py:68
  345.4 11.9 %cholesky.333 = f32[128,128]{1,0:T(8,128)S(1)} custom-call(f32[128,128]{1,0:T(8,128)S(1)} %convolution_subtract_fusion.1), custom_call_target="Cholesky" | custom-call | tf_op jit(solution)/shard_map/jit(cholesky)/cholesky | solution.py:68
  (139 shorter events, 74.7 us)
Async XLA Ops:
  0.0 1.7 copy-start
  0.0 2.4 copy-start.2
  3.2 4.6 %collective-permute-start = (f32[512,64]{0,1:T(8,128)S(1)}, f32[512,64]{0,1:T(8,128)S(1)}, u32[]{:S(2)}, u32[]{:S(2)}) collective-permute-start(f32[512,64]{0,1:T(8,128)S(1)} %pad_maximum_fusion.3), channel_id=1, source_target_pairs={{0,1},{1,0},{2,3},{3,2},{4,5},{5,4},{6,7},{7,6},{8,9},{9,8},{10,11... | collective-permute-start | bytes 393224 | tf_op jit(solution)/shard_map/ppermute | solution.py:21
  7.8 6.1 %collective-permute-start.1 = (f32[512,64]{0,1:T(8,128)S(1)}, f32[512,64]{0,1:T(8,128)S(1)}, u32[]{:S(2)}, u32[]{:S(2)}) collective-permute-start(f32[512,64]{0,1:T(8,128)S(1)} %fusion.87), channel_id=1, source_target_pairs={{0,2},{1,3},{2,0},{3,1},{4,6},{5,7},{6,4},{7,5},{8,10},{9,11},{10,... | collective-permute-start | bytes 393224 | tf_op jit(solution)/shard_map/ppermute | solution.py:21
  13.9 3.9 %collective-permute-start.2 = (f32[512,64]{0,1:T(8,128)S(1)}, f32[512,64]{0,1:T(8,128)S(1)}, u32[]{:S(2)}, u32[]{:S(2)}) collective-permute-start(f32[512,64]{0,1:T(8,128)S(1)} %add.79), channel_id=1, source_target_pairs={{0,4},{4,0},{8,12},{12,8},{1,5},{5,1},{9,13},{13,9},{2,6},{6,2},{1... | collective-permute-start | bytes 393224 | tf_op jit(solution)/shard_map/ppermute | solution.py:21
  17.8 8.2 %collective-permute-start.3 = (f32[1024,64]{0,1:T(8,128)S(1)}, f32[1024,64]{0,1:T(8,128)S(1)}, u32[]{:S(2)}, u32[]{:S(2)}) collective-permute-start(f32[1024,64]{0,1:T(8,128)S(1)} %maximum_select_fusion.3), channel_id=1, source_target_pairs={{0,8},{4,12},{8,0},{12,4},{1,9},{5,13},{9,1},{13,5},{2,10},{6,14},... | collective-permute-start | bytes 786440 | tf_op jit(solution)/shard_map/ppermute | solution.py:21
  57.9 1.0 copy-start.1
  59.0 7.4 %collective-permute-start.4 = (f32[256,512]{1,0:T(8,128)S(1)}, f32[256,512]{1,0:T(8,128)S(1)}, u32[]{:S(2)}, u32[]{:S(2)}) collective-permute-start(f32[256,512]{1,0:T(8,128)S(1)} %slice_select_fusion), channel_id=1, source_target_pairs={{0,16},{16,0},{32,48},{48,32},{64,80},{80,64},{96,112},{112,96},{1... | collective-permute-start | bytes 1572872 | tf_op jit(solution)/shard_map/ppermute | solution.py:21
  67.8 7.6 %collective-permute-start.5 = (f32[128,512]{1,0:T(8,128)S(1)}, f32[128,512]{1,0:T(8,128)S(1)}, u32[]{:S(2)}, u32[]{:S(2)}) collective-permute-start(f32[128,512]{1,0:T(8,128)S(1)} %slice_select_fusion.1), channel_id=1, source_target_pairs={{0,32},{16,48},{32,0},{48,16},{64,96},{80,112},{96,64},{112,80},{1... | collective-permute-start | bytes 786440 | tf_op jit(solution)/shard_map/ppermute | solution.py:21
  75.5 8.7 %collective-permute-start.6 = (f32[64,512]{1,0:T(8,128)S(1)}, f32[64,512]{1,0:T(8,128)S(1)}, u32[]{:S(2)}, u32[]{:S(2)}) collective-permute-start(f32[64,512]{1,0:T(8,128)S(1)} %slice_select_fusion.2), channel_id=1, source_target_pairs={{0,64},{16,80},{32,96},{48,112},{64,0},{80,16},{96,32},{112,48},{1... | collective-permute-start | bytes 393224 | tf_op jit(solution)/shard_map/ppermute | solution.py:21
  84.2 7.3 %collective-permute-start.7 = (f32[32,512]{1,0:T(8,128)S(1)}, f32[32,512]{1,0:T(8,128)S(1)}, u32[]{:S(2)}, u32[]{:S(2)}) collective-permute-start(f32[32,512]{1,0:T(8,128)S(1)} %slice_select_fusion.3), channel_id=1, source_target_pairs={{0,128},{16,144},{32,160},{48,176},{64,192},{80,208},{96,224},{112... | collective-permute-start | bytes 196616 | tf_op jit(solution)/shard_map/ppermute | solution.py:21
  91.5 7.2 %collective-permute-start.8 = (f32[32,512]{1,0:T(8,128)S(1)}, f32[32,512]{1,0:T(8,128)S(1)}, u32[]{:S(2)}, u32[]{:S(2)}) collective-permute-start(f32[32,512]{1,0:T(8,128)S(1)} %select_add_fusion.3), channel_id=1, source_target_pairs={{0,128},{16,144},{32,160},{48,176},{64,192},{80,208},{96,224},{112... | collective-permute-start | bytes 196616 | tf_op jit(solution)/shard_map/ppermute | solution.py:21
  98.8 6.9 %collective-permute-start.9 = (f32[64,512]{1,0:T(8,128)S(1)}, f32[64,512]{1,0:T(8,128)S(1)}, u32[]{:S(2)}, u32[]{:S(2)}) collective-permute-start(f32[64,512]{1,0:T(8,128)S(1)} %maximum_select_fusion.5), channel_id=1, source_target_pairs={{0,64},{16,80},{32,96},{48,112},{64,0},{80,16},{96,32},{112,48},{1... | collective-permute-start | bytes 393224 | tf_op jit(solution)/shard_map/ppermute | solution.py:21
  105.7 6.1 %collective-permute-start.10 = (f32[128,512]{1,0:T(8,128)S(1)}, f32[128,512]{1,0:T(8,128)S(1)}, u32[]{:S(2)}, u32[]{:S(2)}) collective-permute-start(f32[128,512]{1,0:T(8,128)S(1)} %maximum_select_fusion.4), channel_id=1, source_target_pairs={{0,32},{16,48},{32,0},{48,16},{64,96},{80,112},{96,64},{112,80},{1... | collective-permute-start | bytes 786440 | tf_op jit(solution)/shard_map/ppermute | solution.py:21
  111.9 8.1 %copy-start.3 = (f32[256,512]{1,0:T(8,128)}, f32[256,512]{1,0:T(8,128)S(1)}, u32[]{:S(2)}) copy-start(f32[256,512]{1,0:T(8,128)S(1)} %maximum_select_fusion.2) | copy-start | bytes 1572868
  111.9 6.2 %collective-permute-start.11 = (f32[256,512]{1,0:T(8,128)S(1)}, f32[256,512]{1,0:T(8,128)}, u32[]{:S(2)}, u32[]{:S(2)}) collective-permute-start(f32[256,512]{1,0:T(8,128)S(1)} %maximum_select_fusion.2), channel_id=1, source_target_pairs={{0,16},{16,0},{32,48},{48,32},{64,80},{80,64},{96,112},{112,96},{1... | collective-permute-start | bytes 1572872 | tf_op jit(solution)/shard_map/ppermute | solution.py:21
  156.6 27.2 %copy-start.4 = (f32[256,512]{1,0:T(8,128)S(1)}, f32[256,512]{1,0:T(8,128)}, u32[]{:S(2)}) copy-start(f32[256,512]{1,0:T(8,128)} %copy-done.3) | copy-start | bytes 1572868
  160.8 0.6 copy-start.6
  250.3 3.6 copy-start.5

commit v3 on v2

--- a/solution.py
+++ b/solution.py
@@ -58,8 +58,8 @@
     cols = gram.shape[0]
     eye = jnp.eye(RANK, dtype=gram.dtype)
     pick = jnp.concatenate([eye] * (cols // RANK), axis=0)
-    lower = jnp.linalg.cholesky(mm_tn(pick, mm(gram, pick)))
-    coords = solve_lower_t(lower, pick)
+    norms = jnp.sqrt(jnp.sum(pick * mm(gram, pick), axis=0))
+    coords = pick / norms[None, :]
     for turn in range(ITERS):
         image = mm(gram, coords)
         lower = jnp.linalg.cholesky(mm_tn(image, mm(gram, image)))

time: 367 us -> 298 us (0.81)
  other arithmetic: 201 us -> 145 us
  matrix products: 51.7 us -> 45.4 us
  local copies, waits for them, and re-layouts: 24.5 us -> 19.2 us
    another operation x6 -> x0, other arithmetic: 34 us -> none  [merged_coords(): lower = jnp.linalg.cholesky(mm_tn(pick, mm(gram, pick)))]
    another operation x7 -> x5, other arithmetic: 60.3 us -> 39.4 us  [solve_lower_t(): lax.linalg.triangular_solve(lower, block, left_side=False, lower=True, tr...]
    another operation x22 -> x15, local copies, waits for them, and re-layouts: 12.2 us -> 7.62 us  [solve_lower_t(): lax.linalg.triangular_solve(lower, block, left_side=False, lower=True, tr...]
    dot_general x8, matrix products: 20.3 us -> 16.5 us  [mm(): return jnp.matmul(a, b, precision=lax.Precision.HIGHEST)]
    another operation x14 -> x13, other arithmetic: 69.9 us -> 68.9 us  [merged_coords(): lower = jnp.linalg.cholesky(mm_tn(image, mm(gram, image)))]
where the time goes in v3:
time: 298 us; the launch traced here: 295 us
  other arithmetic  145 us (49%)
  waiting for transfers between devices  46.6 us (16%)
  matrix products  45.4 us (15%)
  starting transfers between devices  33.6 us (11%)
  local copies, waits for them, and re-layouts  19.2 us (6%)
  between operations  4.76 us (2%)
    another operation x13, other arithmetic, merged_coords(): lower = jnp.linalg.cholesky(mm_tn(image, mm(gram, image)))  68.9 us
    ppermute x12, waiting for transfers between devices, exchange(): return lax.ppermute(block, axis, [(i, i ^ 1 << bit) for i in range(count)])  46.6 us
    another operation x5, other arithmetic, solve_lower_t(): lax.linalg.triangular_solve(lower, block, left_side=False, lower=True, tr...  39.4 us
    another operation x7, other arithmetic, merged_coords(): lower = jnp.linalg.cholesky(mm_tn(weights, weights))  34.9 us
    ppermute x12, starting transfers between devices, exchange(): return lax.ppermute(block, axis, [(i, i ^ 1 << bit) for i in range(count)])  33.6 us
    dot_general x8, matrix products, mm(): return jnp.matmul(a, b, precision=lax.Precision.HIGHEST)  16.5 us
    dot_general x1, matrix products, shards(): jnp.einsum('etk,etl->ekl', left_all, right_all, precision=lax.Precision.H...  16.5 us
    another operation x15, local copies, waits for them, and re-layouts, solve_lower_t(): lax.linalg.triangular_solve(lower, block, left_side=False, lower=True, tr...  7.62 us
  transfers between devices with their start and end apart: 12, of which 12 were waited for; matrix products, arithmetic and copies ran while one was open for 0% of the time, Pallas kernels for 0%

profile of v3, /device:TPU:1, one launch (start us, length us, event | category | flops | bytes accessed | tf_op | source)
XLA Modules:
  0.0 294.7 jit_solution(11046587630659383628)
XLA Ops:
  5.4 2.4 collective-permute-done
  7.8 3.7 %collective-permute-start.1 = (f32[512,64]{0,1:T(8,128)S(1)}, f32[512,64]{0,1:T(8,128)S(1)}, u32[]{:S(2)}, u32[]{:S(2)}) collective-permute-start(f32[512,64]{0,1:T(8,128)S(1)} %fusion.72), channel_id=1, source_target_pairs={{0,2},{1,3},{2,0},{3,1},{4,6},{5,7},{6,4},{7,5},{8,10},{9,11},{10,... | collective-permute-start | bytes 393224 | tf_op jit(solution)/shard_map/ppermute | solution.py:21
  11.5 2.4 collective-permute-done.1
  15.2 2.6 collective-permute-done.2
  17.8 3.1 %collective-permute-start.3 = (f32[1024,64]{0,1:T(8,128)S(1)}, f32[1024,64]{0,1:T(8,128)S(1)}, u32[]{:S(2)}, u32[]{:S(2)}) collective-permute-start(f32[1024,64]{0,1:T(8,128)S(1)} %maximum_select_fusion.3), channel_id=1, source_target_pairs={{0,8},{4,12},{8,0},{12,4},{1,9},{5,13},{9,1},{13,5},{2,10},{6,14},... | collective-permute-start | bytes 786440 | tf_op jit(solution)/shard_map/ppermute | solution.py:21
  20.9 5.1 %collective-permute-done.3 = f32[1024,64]{0,1:T(8,128)S(1)} collective-permute-done((f32[1024,64]{0,1:T(8,128)S(1)}, f32[1024,64]{0,1:T(8,128)S(1)}, u32[]{:S(2)}, u32[]{:S(2)}) %collective-permute-start.3) | collective-permute-done | bytes 262176 | tf_op jit(solution)/shard_map/ppermute | solution.py:21
  29.4 16.5 %fusion.79 = f32[512,32,32]{2,1,0:T(8,128)} fusion(f32[512,4,32]{2,1,0:T(4,128)S(1)} %bitcast.127, f32[512,4,32]{2,1,0:T(4,128)} %bitcast.128), kind=kOutput, calls=%fused_computation.138 | convolution fusion | flops 25165824 | bytes 2621440 | tf_op jit(solution)/shard_map/etk,etl->ekl/dot_general | solution.py:93
  45.9 6.3 %copy.25 = f32[512,32,32]{0,2,1:T(8,128)} copy(f32[512,32,32]{2,1,0:T(8,128)} %fusion.79) | data formatting | bytes 4194304 | tf_op jit(solution)/shard_map/etk,etl->ekl/dot_general | solution.py:93
  52.2 5.8 %convolution_bitcast_fusion = f32[512,512]{1,0:T(8,128)S(1)} fusion(f32[512,32,32]{0,2,1:T(8,128)} %copy.25), kind=kOutput, calls=%fused_computation.8 | convolution fusion | flops 3221225472 | bytes 3145728 | tf_op jit(solution)/shard_map/dot_general | solution.py:12
  59.0 5.9 %collective-permute-start.4 = (f32[256,512]{1,0:T(8,128)S(1)}, f32[256,512]{1,0:T(8,128)S(1)}, u32[]{:S(2)}, u32[]{:S(2)}) collective-permute-start(f32[256,512]{1,0:T(8,128)S(1)} %slice_select_fusion), channel_id=1, source_target_pairs={{0,16},{16,0},{32,48},{48,32},{64,80},{80,64},{96,112},{112,96},{1... | collective-permute-start | bytes 1572872 | tf_op jit(solution)/shard_map/ppermute | solution.py:21
  68.0 7.5 %collective-permute-done.5 = f32[128,512]{1,0:T(8,128)S(1)} collective-permute-done((f32[128,512]{1,0:T(8,128)S(1)}, f32[128,512]{1,0:T(8,128)S(1)}, u32[]{:S(2)}, u32[]{:S(2)}) %collective-permute-start.5) | collective-permute-done | bytes 262176 | tf_op jit(solution)/shard_map/ppermute | solution.py:21
  77.2 7.2 %collective-permute-done.6 = f32[64,512]{1,0:T(8,128)S(1)} collective-permute-done((f32[64,512]{1,0:T(8,128)S(1)}, f32[64,512]{1,0:T(8,128)S(1)}, u32[]{:S(2)}, u32[]{:S(2)}) %collective-permute-start.6) | collective-permute-done | bytes 131104 | tf_op jit(solution)/shard_map/ppermute | solution.py:21
  84.5 5.2 %collective-permute-start.7 = (f32[32,512]{1,0:T(8,128)S(1)}, f32[32,512]{1,0:T(8,128)S(1)}, u32[]{:S(2)}, u32[]{:S(2)}) collective-permute-start(f32[32,512]{1,0:T(8,128)S(1)} %slice_select_fusion.3), channel_id=1, source_target_pairs={{0,128},{16,144},{32,160},{48,176},{64,192},{80,208},{96,224},{112... | collective-permute-start | bytes 196616 | tf_op jit(solution)/shard_map/ppermute | solution.py:21
  91.6 5.2 %collective-permute-start.8 = (f32[32,512]{1,0:T(8,128)S(1)}, f32[32,512]{1,0:T(8,128)S(1)}, u32[]{:S(2)}, u32[]{:S(2)}) collective-permute-start(f32[32,512]{1,0:T(8,128)S(1)} %select_add_fusion.3), channel_id=1, source_target_pairs={{0,128},{16,144},{32,160},{48,176},{64,192},{80,208},{96,224},{112... | collective-permute-start | bytes 196616 | tf_op jit(solution)/shard_map/ppermute | solution.py:21
  98.9 6.5 %collective-permute-done.9 = f32[64,512]{1,0:T(8,128)S(1)} collective-permute-done((f32[64,512]{1,0:T(8,128)S(1)}, f32[64,512]{1,0:T(8,128)S(1)}, u32[]{:S(2)}, u32[]{:S(2)}) %collective-permute-start.9) | collective-permute-done | bytes 131104 | tf_op jit(solution)/shard_map/ppermute | solution.py:21
  105.5 6.0 %collective-permute-done.10 = f32[128,512]{1,0:T(8,128)S(1)} collective-permute-done((f32[128,512]{1,0:T(8,128)S(1)}, f32[128,512]{1,0:T(8,128)S(1)}, u32[]{:S(2)}, u32[]{:S(2)}) %collective-permute-start.10) | collective-permute-done | bytes 262176 | tf_op jit(solution)/shard_map/ppermute | solution.py:21
  111.6 5.0 %collective-permute-start.11 = (f32[256,512]{1,0:T(8,128)S(1)}, f32[256,512]{1,0:T(8,128)S(1)}, u32[]{:S(2)}, u32[]{:S(2)}) collective-permute-start(f32[256,512]{1,0:T(8,128)S(1)} %maximum_select_fusion.2), channel_id=1, source_target_pairs={{0,16},{16,0},{32,48},{48,32},{64,80},{80,64},{96,112},{112,96},{1... | collective-permute-start | bytes 1572872 | tf_op jit(solution)/shard_map/ppermute | solution.py:21
  123.5 11.7 %cholesky.172 = f32[128,128]{1,0:T(8,128)S(1)} custom-call(f32[128,128]{1,0:T(8,128)S(1)} %cholesky.270), custom_call_target="Cholesky" | custom-call | tf_op jit(solution)/shard_map/jit(cholesky)/cholesky | solution.py:65
  135.3 9.8 %custom-call.14 = f32[1,128,128]{1,2,0:T(8,128)S(1)} custom-call(f32[1,128,128]{2,1,0:T(8,128)S(1)} %get-tuple-element.58), custom_call_target="InvertDiagBlocksLowerTriangular" | custom-call | tf_op jit(solution)/shard_map/jit(cholesky)/cholesky | solution.py:65
  145.6 11.9 %cholesky.189 = f32[128,128]{1,0:T(8,128)S(1)} custom-call(f32[128,128]{1,0:T(8,128)S(1)} %convolution_subtract_fusion.2), custom_call_target="Cholesky" | custom-call | tf_op jit(solution)/shard_map/jit(cholesky)/cholesky | solution.py:65
  159.5 3.8 %while.4 = (s32[]{:T(128)}, f32[256,256]{1,0:T(8,128)S(1)}, s32[2,2]{1,0:T(2,128)S(1)}, f32[2,128,128]{2,1,0:T(8,128)S(1)}, s32[]{:T(128)}) while((s32[]{:T(128)}, f32[256,256]{1,0:T(8,128)S(1)}, s32[2,2]{1,0:T(2,128)S(1)}, f32[2,128,128]{2,1,0:T(8,128)S(1)}, s32[]{:T(128)}) %tuple.48), condition=%wide.while_cond, body=%wide.while_body.sunk | while | flops 2 | bytes 131181 | solution.py:54
  163.3 19.7 %custom-call.15 = f32[2,128,128]{1,2,0:T(8,128)S(1)} custom-call(f32[2,128,128]{2,1,0:T(8,128)S(1)} %get-tuple-element.21), custom_call_target="InvertDiagBlocksLowerTriangular" | custom-call | tf_op jit(solution)/shard_map/triangular_solve/custom-call.0 | solution.py:54
  184.5 2.6 fusion.11
  189.2 11.7 %cholesky.206 = f32[128,128]{1,0:T(8,128)S(1)} custom-call(f32[128,128]{1,0:T(8,128)S(1)} %cholesky.273), custom_call_target="Cholesky" | custom-call | tf_op jit(solution)/shard_map/jit(cholesky)/cholesky | solution.py:65
  201.0 9.8 %custom-call.16 = f32[1,128,128]{1,2,0:T(8,128)S(1)} custom-call(f32[1,128,128]{2,1,0:T(8,128)S(1)} %get-tuple-element.54), custom_call_target="InvertDiagBlocksLowerTriangular" | custom-call | tf_op jit(solution)/shard_map/jit(cholesky)/cholesky | solution.py:65
  211.3 11.9 %cholesky.223 = f32[128,128]{1,0:T(8,128)S(1)} custom-call(f32[128,128]{1,0:T(8,128)S(1)} %convolution_subtract_fusion.1), custom_call_target="Cholesky" | custom-call | tf_op jit(solution)/shard_map/jit(cholesky)/cholesky | solution.py:65
  225.8 3.8 %while.5 = (s32[]{:T(128)}, f32[256,256]{1,0:T(8,128)S(1)}, s32[2,2]{1,0:T(2,128)S(1)}, f32[2,128,128]{2,1,0:T(8,128)S(1)}, s32[]{:T(128)}) while((s32[]{:T(128)}, f32[256,256]{1,0:T(8,128)S(1)}, s32[2,2]{1,0:T(2,128)S(1)}, f32[2,128,128]{2,1,0:T(8,128)S(1)}, s32[]{:T(128)}) %tuple.54), condition=%wide.while_cond.clone, body=%wide.while_body.clone.sunk | while | flops 2 | bytes 131181 | solution.py:54
  229.6 19.7 %custom-call.17 = f32[2,128,128]{1,2,0:T(8,128)S(1)} custom-call(f32[2,128,128]{2,1,0:T(8,128)S(1)} %get-tuple-element.22), custom_call_target="InvertDiagBlocksLowerTriangular" | custom-call | tf_op jit(solution)/shard_map/triangular_solve/custom-call.0 | solution.py:54
  250.8 2.6 fusion.21
  254.6 11.7 %cholesky.240 = f32[128,128]{1,0:T(8,128)S(1)} custom-call(f32[128,128]{1,0:T(8,128)S(1)} %cholesky.276), custom_call_target="Cholesky" | custom-call | tf_op jit(solution)/shard_map/jit(cholesky)/cholesky | solution.py:68
  266.3 9.8 %custom-call.18 = f32[1,128,128]{1,2,0:T(8,128)S(1)} custom-call(f32[1,128,128]{2,1,0:T(8,128)S(1)} %get-tuple-element.50), custom_call_target="InvertDiagBlocksLowerTriangular" | custom-call | tf_op jit(solution)/shard_map/jit(cholesky)/cholesky | solution.py:68
  276.6 11.9 %cholesky.257 = f32[128,128]{1,0:T(8,128)S(1)} custom-call(f32[128,128]{1,0:T(8,128)S(1)} %convolution_subtract_fusion), custom_call_target="Cholesky" | custom-call | tf_op jit(solution)/shard_map/jit(cholesky)/cholesky | solution.py:68
  (114 shorter events, 49.1 us)
Async XLA Ops:
  0.0 1.7 copy-start
  0.0 2.4 copy-start.2
  3.2 4.6 %collective-permute-start = (f32[512,64]{0,1:T(8,128)S(1)}, f32[512,64]{0,1:T(8,128)S(1)}, u32[]{:S(2)}, u32[]{:S(2)}) collective-permute-start(f32[512,64]{0,1:T(8,128)S(1)} %pad_maximum_fusion.3), channel_id=1, source_target_pairs={{0,1},{1,0},{2,3},{3,2},{4,5},{5,4},{6,7},{7,6},{8,9},{9,8},{10,11... | collective-permute-start | bytes 393224 | tf_op jit(solution)/shard_map/ppermute | solution.py:21
  7.8 6.1 %collective-permute-start.1 = (f32[512,64]{0,1:T(8,128)S(1)}, f32[512,64]{0,1:T(8,128)S(1)}, u32[]{:S(2)}, u32[]{:S(2)}) collective-permute-start(f32[512,64]{0,1:T(8,128)S(1)} %fusion.72), channel_id=1, source_target_pairs={{0,2},{1,3},{2,0},{3,1},{4,6},{5,7},{6,4},{7,5},{8,10},{9,11},{10,... | collective-permute-start | bytes 393224 | tf_op jit(solution)/shard_map/ppermute | solution.py:21
  13.9 3.9 %collective-permute-start.2 = (f32[512,64]{0,1:T(8,128)S(1)}, f32[512,64]{0,1:T(8,128)S(1)}, u32[]{:S(2)}, u32[]{:S(2)}) collective-permute-start(f32[512,64]{0,1:T(8,128)S(1)} %add.79), channel_id=1, source_target_pairs={{0,4},{4,0},{8,12},{12,8},{1,5},{5,1},{9,13},{13,9},{2,6},{6,2},{1... | collective-permute-start | bytes 393224 | tf_op jit(solution)/shard_map/ppermute | solution.py:21
  17.8 8.2 %collective-permute-start.3 = (f32[1024,64]{0,1:T(8,128)S(1)}, f32[1024,64]{0,1:T(8,128)S(1)}, u32[]{:S(2)}, u32[]{:S(2)}) collective-permute-start(f32[1024,64]{0,1:T(8,128)S(1)} %maximum_select_fusion.3), channel_id=1, source_target_pairs={{0,8},{4,12},{8,0},{12,4},{1,9},{5,13},{9,1},{13,5},{2,10},{6,14},... | collective-permute-start | bytes 786440 | tf_op jit(solution)/shard_map/ppermute | solution.py:21
  57.9 1.0 copy-start.1
  59.0 7.4 %collective-permute-start.4 = (f32[256,512]{1,0:T(8,128)S(1)}, f32[256,512]{1,0:T(8,128)S(1)}, u32[]{:S(2)}, u32[]{:S(2)}) collective-permute-start(f32[256,512]{1,0:T(8,128)S(1)} %slice_select_fusion), channel_id=1, source_target_pairs={{0,16},{16,0},{32,48},{48,32},{64,80},{80,64},{96,112},{112,96},{1... | collective-permute-start | bytes 1572872 | tf_op jit(solution)/shard_map/ppermute | solution.py:21
  67.8 7.6 %collective-permute-start.5 = (f32[128,512]{1,0:T(8,128)S(1)}, f32[128,512]{1,0:T(8,128)S(1)}, u32[]{:S(2)}, u32[]{:S(2)}) collective-permute-start(f32[128,512]{1,0:T(8,128)S(1)} %slice_select_fusion.1), channel_id=1, source_target_pairs={{0,32},{16,48},{32,0},{48,16},{64,96},{80,112},{96,64},{112,80},{1... | collective-permute-start | bytes 786440 | tf_op jit(solution)/shard_map/ppermute | solution.py:21
  75.5 8.9 %collective-permute-start.6 = (f32[64,512]{1,0:T(8,128)S(1)}, f32[64,512]{1,0:T(8,128)S(1)}, u32[]{:S(2)}, u32[]{:S(2)}) collective-permute-start(f32[64,512]{1,0:T(8,128)S(1)} %slice_select_fusion.2), channel_id=1, source_target_pairs={{0,64},{16,80},{32,96},{48,112},{64,0},{80,16},{96,32},{112,48},{1... | collective-permute-start | bytes 393224 | tf_op jit(solution)/shard_map/ppermute | solution.py:21
  84.5 7.1 %collective-permute-start.7 = (f32[32,512]{1,0:T(8,128)S(1)}, f32[32,512]{1,0:T(8,128)S(1)}, u32[]{:S(2)}, u32[]{:S(2)}) collective-permute-start(f32[32,512]{1,0:T(8,128)S(1)} %slice_select_fusion.3), channel_id=1, source_target_pairs={{0,128},{16,144},{32,160},{48,176},{64,192},{80,208},{96,224},{112... | collective-permute-start | bytes 196616 | tf_op jit(solution)/shard_map/ppermute | solution.py:21
  91.6 7.2 %collective-permute-start.8 = (f32[32,512]{1,0:T(8,128)S(1)}, f32[32,512]{1,0:T(8,128)S(1)}, u32[]{:S(2)}, u32[]{:S(2)}) collective-permute-start(f32[32,512]{1,0:T(8,128)S(1)} %select_add_fusion.3), channel_id=1, source_target_pairs={{0,128},{16,144},{32,160},{48,176},{64,192},{80,208},{96,224},{112... | collective-permute-start | bytes 196616 | tf_op jit(solution)/shard_map/ppermute | solution.py:21
  98.8 6.6 %collective-permute-start.9 = (f32[64,512]{1,0:T(8,128)S(1)}, f32[64,512]{1,0:T(8,128)S(1)}, u32[]{:S(2)}, u32[]{:S(2)}) collective-permute-start(f32[64,512]{1,0:T(8,128)S(1)} %maximum_select_fusion.5), channel_id=1, source_target_pairs={{0,64},{16,80},{32,96},{48,112},{64,0},{80,16},{96,32},{112,48},{1... | collective-permute-start | bytes 393224 | tf_op jit(solution)/shard_map/ppermute | solution.py:21
  105.4 6.1 %collective-permute-start.10 = (f32[128,512]{1,0:T(8,128)S(1)}, f32[128,512]{1,0:T(8,128)S(1)}, u32[]{:S(2)}, u32[]{:S(2)}) collective-permute-start(f32[128,512]{1,0:T(8,128)S(1)} %maximum_select_fusion.4), channel_id=1, source_target_pairs={{0,32},{16,48},{32,0},{48,16},{64,96},{80,112},{96,64},{112,80},{1... | collective-permute-start | bytes 786440 | tf_op jit(solution)/shard_map/ppermute | solution.py:21
  111.6 9.7 %copy-start.3 = (f32[256,512]{1,0:T(8,128)}, f32[256,512]{1,0:T(8,128)S(1)}, u32[]{:S(2)}) copy-start(f32[256,512]{1,0:T(8,128)S(1)} %maximum_select_fusion.2) | copy-start | bytes 1572868
  111.6 6.5 %collective-permute-start.11 = (f32[256,512]{1,0:T(8,128)S(1)}, f32[256,512]{1,0:T(8,128)S(1)}, u32[]{:S(2)}, u32[]{:S(2)}) collective-permute-start(f32[256,512]{1,0:T(8,128)S(1)} %maximum_select_fusion.2), channel_id=1, source_target_pairs={{0,16},{16,0},{32,48},{48,32},{64,80},{80,64},{96,112},{112,96},{1... | collective-permute-start | bytes 1572872 | tf_op jit(solution)/shard_map/ppermute | solution.py:21
  118.2 0.8 copy-start.5
  119.0 2.3 copy-start.6
  183.4 3.6 %copy-start.4 = (f32[256,512]{1,0:T(8,128)S(1)}, f32[256,512]{1,0:T(8,128)}, u32[]{:S(2)}) copy-start(f32[256,512]{1,0:T(8,128)} %copy-done.3) | copy-start | bytes 1572868
  183.4 3.6 %copy-start.7 = (f32[256,512]{1,0:T(8,128)S(1)}, f32[256,512]{1,0:T(8,128)}, u32[]{:S(2)}) copy-start(f32[256,512]{1,0:T(8,128)} %copy-done.5) | copy-start | bytes 1572868
